TPU v7x, 32 devices: a whole 2x2x4 slice. The times are simulated.
32 devices in a mesh: row: 8 (over z, y), col: 4 (over x, core).
Axes of the slice: x: 2, y: 2, z: 4, core: 2. Of those that a mesh axis runs over, the one named last changes fastest.
Arguments:
- tokens: bfloat16 [384, 8192], P('row', 'col'), may hold values from -6 to 6
- weight: bfloat16 [8192, 32768], P('col', 'row'), may hold values from -0.109375 to 0.109375
- tile_rows: int32 [8, 4, 256], P('row', 'col'), may hold values from 0 to 63, as said below
- tile_cols: int32 [8, 4, 256], P('row', 'col'), may hold values from 0 to 255, as said below
- tile_count: int32 [8, 4], P('row', 'col'), may hold values from 64 to 256, as said below
- hidden_cotangent: bfloat16 [384, 32768], P('col', 'row'), may hold values from -6 to 6
Outputs:
- hidden: bfloat16 [384, 32768], P('col', 'row')
- input_grad: bfloat16 [384, 8192], P('row', 'col')
- weight_grad: bfloat16 [8192, 32768], P('col', 'row')
Inputs may be any that keep to these rules, and one draw needn't show every extreme that they name: tile_rows[r, c, k] is a row block of the weight (tiles of 128 x 128) among the 16 blocks from c * 16 on, which index c of col holds. tile_cols[r, c, k] is a column block among the 32 blocks from r * 32 on, which index r of row holds; the 256 candidate tiles of one device are distinct. The first tile_count[r, c] candidates of device (r, c) are its nonzero tiles; some device holds 256.
All inputs are finite; a program needn't handle non-finite values.
Results may differ from a plain program's by a relative error of at most 0.0049.
Values may be sent and summed in bfloat16 or wider, within the bound.
A program may use at most 128 MiB of HBM per device.

v0:
```python
import jax
import jax.numpy as jnp
from jax import lax
from jax.sharding import PartitionSpec as P

TILE = 128


def exchange_sum(partial, axis):
    n = lax.psum(1, axis)
    rows = partial.shape[0] // n
    mine = lax.all_to_all(
        partial.reshape(n, rows, partial.shape[1]), axis, split_axis=0, concat_axis=0
    )
    return mine.astype(jnp.float32).sum(axis=0)


def on_device(tokens, weight, tile_rows, tile_cols, tile_count, hidden_cotangent):
    row_index = lax.axis_index("row")
    col_index = lax.axis_index("col")
    row_blocks = weight.shape[0] // TILE
    col_blocks = weight.shape[1] // TILE
    capacity = tile_rows.shape[2]
    local_rows = tile_rows.reshape(capacity) - col_index * row_blocks
    local_cols = tile_cols.reshape(capacity) - row_index * col_blocks
    is_live = jnp.arange(capacity) < tile_count.reshape(())
    row_pick = ((local_rows[None, :] == jnp.arange(row_blocks)[:, None]) & is_live[None, :]).astype(
        jnp.bfloat16
    )
    col_pick = (local_cols[:, None] == (jnp.arange(weight.shape[1]) // TILE)[None, :]).astype(
        jnp.bfloat16
    )
    mask = jnp.dot(row_pick, col_pick, preferred_element_type=jnp.float32)
    live = (mask > 0.5)[:, None, :]
    shaped = weight.reshape(row_blocks, TILE, weight.shape[1])
    masked = jnp.where(live, shaped, jnp.zeros_like(shaped)).reshape(weight.shape)
    full_tokens = lax.all_gather(tokens, "row", axis=0, tiled=True)
    partial = jnp.dot(full_tokens, masked, preferred_element_type=jnp.float32)
    pre_act = exchange_sum(partial.astype(jnp.bfloat16), "col")
    gate_value = jax.nn.sigmoid(pre_act)
    hidden = (pre_act * gate_value).astype(jnp.bfloat16)
    silu_slope = gate_value * (1.0 + pre_act * (1.0 - gate_value))
    grad_pre = (hidden_cotangent.astype(jnp.float32) * silu_slope).astype(jnp.bfloat16)
    full_grads = lax.all_gather(grad_pre, "col", axis=0, tiled=True)
    share = lax.dot_general(
        full_grads, masked, (((1,), (1,)), ((), ())), preferred_element_type=jnp.float32
    )
    input_grad = exchange_sum(share.astype(jnp.bfloat16), "row").astype(jnp.bfloat16)
    full = lax.dot_general(
        full_tokens, full_grads, (((0,), (0,)), ((), ())), preferred_element_type=jnp.float32
    ).reshape(row_blocks, TILE, weight.shape[1])
    weight_grad = jnp.where(live, full, 0.0).astype(jnp.bfloat16).reshape(weight.shape)
    return (hidden, input_grad, weight_grad)


def solution(mesh):
    in_specs = (
        P("row", "col"),
        P("col", "row"),
        P("row", "col", None),
        P("row", "col", None),
        P("row", "col"),
        P("col", "row"),
    )
    out_specs = (P("col", "row"), P("row", "col"), P("col", "row"))
    return jax.shard_map(
        on_device, mesh=mesh, in_specs=in_specs, out_specs=out_specs, check_vma=False
    )
```

profile of v0, /device:TPU:0, one launch (start us, length us, event | category | flops | bytes accessed | tf_op | source)
XLA Modules:
  0.0 230.9 jit_solution(18191495320413865887)
XLA Ops:
  7.2 0.0 all-gather.3.cloned.1.call-start
  7.2 0.7 all-gather.3.cloned.1.call-update
  7.9 0.0 all-gather.5.cloned.1.call-start
  8.6 0.7 broadcast_subtract_fusion.1
  9.3 0.7 broadcast_subtract_fusion
  10.0 0.8 convolution_compare_fusion
  10.8 0.8 copy.9
  11.6 22.5 %copy.10 = bf16[2048,4096]{0,1:T(8,128)(2,1)} copy(bf16[2048,4096]{1,0:T(8,128)(2,1)} %param.7) | data formatting | bytes 33554432 | tf_op args[1]
  34.1 23.0 %all-gather.3.cloned.1.call-done = bf16[384,2048]{1,0:T(8,128)(2,1)} async-done(((bf16[48,2048]{1,0:T(8,128)(2,1)}), bf16[384,2048]{1,0:T(8,128)(2,1)}) %all-gather.3.cloned.1.call-update) | async-done | bytes 1572880 | tf_op jit(solution)/shard_map/all_gather | solution.py:37
  57.1 26.5 %broadcast_in_dim.29 = pred[16,128,4096]{1,0,2:T(8,128)(4,1)S(1)} broadcast(pred[16,4096]{0,1:T(8,128)(4,1)S(1)} %copy.9), dimensions={0,2} | broadcast | bytes 8454144 | tf_op jit(solution)/shard_map/jit(_where)/broadcast_in_dim | solution.py:36
  83.6 0.0 copy-start
  83.6 13.5 %fusion.5 = bf16[4096,384]{0,1:T(8,128)(2,1)S(1)} fusion(bf16[384,2048]{1,0:T(8,128)(2,1)S(1)} %copy-done.2, bf16[2048,4096]{0,1:T(8,128)(2,1)} %copy.10, pred[512,8,16,128]{3,2,1,0:T(8,128)(4,1)S(1)} %bitcast.28), kind=kOutput, calls=%fused_computation.8 | convolution fusion | flops 6452412416 | bytes 29884416 | tf_op jit(solution)/shard_map/dot_general | solution.py:38
  97.2 39.4 %all_to_all.10 = bf16[4,96,4096]{2,1,0:T(8,128)(2,1)S(1)} all-to-all(bf16[4,96,4096]{2,1,0:T(8,128)(2,1)S(1)} %bitcast.31), channel_id=1, replica_groups=mesh['row'=8,'col'=4] {'col'}, dimensions={0} | all-to-all | bytes 6291456 | tf_op jit(solution)/shard_map/all_to_all | solution.py:12
  136.6 0.5 convert_reduce_fusion
  137.1 0.6 copy-done.1
  137.8 1.8 multiply_convert_fusion
  139.6 0.0 all-gather.5.cloned.1.call-update
  139.6 26.1 %all-gather.5.cloned.1.call-done = bf16[384,4096]{1,0:T(8,128)(2,1)} async-done(((bf16[96,4096]{1,0:T(8,128)(2,1)}), bf16[384,4096]{1,0:T(8,128)(2,1)}) %all-gather.5.cloned.1.call-update) | async-done | bytes 3145744 | tf_op jit(solution)/shard_map/all_gather | solution.py:44
  165.7 13.5 %fusion.7 = bf16[384,2048]{1,0:T(8,128)(2,1)} fusion(bf16[384,4096]{1,0:T(8,128)(2,1)} %all-gather.5.cloned.1.call-done, bf16[2048,4096]{0,1:T(8,128)(2,1)} %copy.10, pred[512,8,16,128]{3,2,1,0:T(8,128)(4,1)} %bitcast.29), kind=kOutput, calls=%fused_computation.11 | convolution fusion | flops 6451625984 | bytes 29884416 | tf_op jit(solution)/shard_map/dot_general | solution.py:45
  179.2 5.5 %all-to-all-start.1 = ((bf16[8,48,2048]{2,1,0:T(8,128)(2,1)}), bf16[8,48,2048]{2,1,0:T(8,128)(2,1)S(1)}, u32[]{:S(2)}, u32[]{:S(2)}) async-start(bf16[8,48,2048]{2,1,0:T(8,128)(2,1)} %bitcast.5), calls=%async_computation.1 | async-start | bytes 3145728 | tf_op jit(solution)/shard_map/all_to_all | solution.py:12
  184.7 17.3 %fusion = bf16[2048,4096]{0,1:T(8,128)(2,1)} fusion(pred[512,8,16,128]{3,2,1,0:T(8,128)(4,1)} %bitcast.30, bf16[384,4096]{1,0:T(8,128)(2,1)} %all-gather.5.cloned.1.call-done, bf16[384,2048]{1,0:T(8,128)(2,1)S(1)} %copy-done.2), kind=kOutput, calls=%fused_computation.1 | convolution fusion | flops 6459228160 | bytes 29884416 | tf_op jit(solution)/shard_map/dot_general | solution.py:49
  201.9 21.2 %copy.11 = bf16[2048,4096]{1,0:T(8,128)(2,1)} copy(bf16[2048,4096]{0,1:T(8,128)(2,1)} %fusion) | data formatting | bytes 33554432
  223.1 0.0 all-to-all-done.1
  223.1 0.9 reduce_sum.22
  (6 shorter events, 0.0 us)
Async XLA Ops:
  7.2 49.9 %all-gather.3.cloned.1.call-start = ((), (), s32[]{:S(2)}) async-start(), calls=%async_computation.2 | async-start | bytes 1769472 | tf_op jit(solution)/shard_map/all_gather | solution.py:37
  7.9 157.8 %all-gather.5.cloned.1.call-start = ((), (), s32[]{:S(2)}) async-start(), calls=%async_computation.3 | async-start | bytes 3932160 | tf_op jit(solution)/shard_map/all_gather | solution.py:44
  57.1 26.5 %copy-start.2 = (bf16[384,2048]{1,0:T(8,128)(2,1)S(1)}, bf16[384,2048]{1,0:T(8,128)(2,1)}, u32[]{:S(2)}) copy-start(bf16[384,2048]{1,0:T(8,128)(2,1)} %all-gather.3.cloned.1.call-done) | copy-start | bytes 4718596
  83.6 13.6 %copy-start = (pred[16,128,4096]{1,0,2:T(8,128)(4,1)}, pred[16,128,4096]{1,0,2:T(8,128)(4,1)S(1)}, u32[]{:S(2)}) copy-start(pred[16,128,4096]{1,0,2:T(8,128)(4,1)S(1)} %broadcast_in_dim.29) | copy-start | bytes 25165828
  136.6 1.1 copy-start.1
  179.2 44.0 %all-to-all-start.1 = ((bf16[8,48,2048]{2,1,0:T(8,128)(2,1)}), bf16[8,48,2048]{2,1,0:T(8,128)(2,1)S(1)}, u32[]{:S(2)}, u32[]{:S(2)}) async-start(bf16[8,48,2048]{2,1,0:T(8,128)(2,1)} %bitcast.5), calls=%async_computation.1 | async-start | bytes 3145728 | tf_op jit(solution)/shard_map/all_to_all | solution.py:12
Sparse Core Ops, SparseCore 0:
  10.2 46.8 all-gather.2
  139.7 25.9 all-gather.4
where the time goes:
time: 232 us; the launch traced here: 231 us
  local copies, waits for them, and re-layouts  71.6 us (31%)
  waiting for transfers between devices  49.8 us (21%)
  matrix products  45 us (19%)
  blocking collectives  39.4 us (17%)
  between operations  14.8 us (6%)
  starting transfers between devices  5.59 us (2%)
  other arithmetic  4.66 us (2%)
    unnamed x8, local copies, waits for them, and re-layouts  44.3 us
    all_to_all x1, blocking collectives, exchange_sum(): lax.all_to_all(partial.reshape(n, rows, partial.shape[1]), axis, split_ax...  39.4 us
    broadcast_in_dim x1, local copies, waits for them, and re-layouts, on_device(): jnp.where(live, shaped, jnp.zeros_like(shaped)).reshape(weight.shape)  26.5 us
    all_gather x1, waiting for transfers between devices, on_device(): full_grads = lax.all_gather(grad_pre, 'col', axis=0, tiled=True)  26.1 us
    all_gather x1, waiting for transfers between devices, on_device(): full_tokens = lax.all_gather(tokens, 'row', axis=0, tiled=True)  23 us
    dot_general x1, matrix products, on_device(): lax.dot_general(full_tokens, full_grads, (((0,), (0,)), ((), ())), prefer...  17.3 us
    dot_general x1, matrix products, on_device(): partial = jnp.dot(full_tokens, masked, preferred_element_type=jnp.float32)  13.5 us
    dot_general x1, matrix products, on_device(): lax.dot_general(full_grads, masked, (((1,), (1,)), ((), ())), preferred_e...  13.5 us
  transfers between devices with their start and end apart: 3, of which 2 were waited for; matrix products, arithmetic and copies ran while one was open for 28% of the time, Pallas kernels for 0%

commit v1 on v0

--- a/solution.py
+++ b/solution.py
@@ -4,6 +4,17 @@
 from jax.sharding import PartitionSpec as P
 
 TILE = 128
+
+
+def around_the_ring(x, mesh_axis, d):
+    count = lax.axis_size(mesh_axis)
+    right = [(i, (i + 1) % count) for i in range(count)]
+    parts = [x]
+    for reach in range(1, count):
+        parts = [lax.ppermute(parts[0], mesh_axis, right), *parts]
+    whole = jnp.concatenate(parts, axis=d)
+    turn = (lax.axis_index(mesh_axis) + 1) * parts[-1].shape[d]
+    return jnp.roll(whole, turn, axis=d)
 
 
 def exchange_sum(partial, axis):
@@ -41,7 +52,7 @@
     hidden = (pre_act * gate_value).astype(jnp.bfloat16)
     silu_slope = gate_value * (1.0 + pre_act * (1.0 - gate_value))
     grad_pre = (hidden_cotangent.astype(jnp.float32) * silu_slope).astype(jnp.bfloat16)
-    full_grads = lax.all_gather(grad_pre, "col", axis=0, tiled=True)
+    full_grads = around_the_ring(grad_pre, "col", 0)
     share = lax.dot_general(
         full_grads, masked, (((1,), (1,)), ((), ())), preferred_element_type=jnp.float32
     )

time: 232 us -> 241 us (1.039)
  waiting for transfers between devices: 49.8 us -> 58 us
  matrix products: 45 us -> 47.9 us
    ppermute x0 -> x3, waiting for transfers between devices: none -> 34.2 us  [around_the_ring(): parts = [lax.ppermute(parts[0], mesh_axis, right), *parts]]
    all_gather x1 -> x0, waiting for transfers between devices: 26.1 us -> none  [on_device(): full_grads = lax.all_gather(grad_pre, 'col', axis=0, tiled=True)]
    unnamed x8 -> x19, local copies, waits for them, and re-layouts: 44.3 us -> 44.1 us
  transfers between devices with their start and end apart: 3 -> 5, of which waited for: 2 -> 4; matrix products, arithmetic and copies ran while one was open for 28% -> 27% of each run, Pallas kernels for 0% -> 0%
where the time goes in v1:
time: 241 us; the launch traced here: 240 us
  local copies, waits for them, and re-layouts  71.4 us (30%)
  waiting for transfers between devices  58 us (24%)
  matrix products  47.9 us (20%)
  blocking collectives  39.6 us (16%)
  between operations  14.9 us (6%)
  other arithmetic  4.39 us (2%)
  starting transfers between devices  3.63 us (2%)
    unnamed x19, local copies, waits for them, and re-layouts  44.1 us
    all_to_all x1, blocking collectives, exchange_sum(): lax.all_to_all(partial.reshape(n, rows, partial.shape[1]), axis, split_ax...  39.6 us
    ppermute x3, waiting for transfers between devices, around_the_ring(): parts = [lax.ppermute(parts[0], mesh_axis, right), *parts]  34.2 us
    broadcast_in_dim x1, local copies, waits for them, and re-layouts, on_device(): jnp.where(live, shaped, jnp.zeros_like(shaped)).reshape(weight.shape)  26.5 us
    all_gather x1, waiting for transfers between devices, on_device(): full_tokens = lax.all_gather(tokens, 'row', axis=0, tiled=True)  23 us
    dot_general x1, matrix products, on_device(): lax.dot_general(full_tokens, full_grads, (((0,), (0,)), ((), ())), prefer...  18.1 us
    dot_general x1, matrix products, on_device(): lax.dot_general(full_grads, masked, (((1,), (1,)), ((), ())), preferred_e...  15.5 us
    dot_general x1, matrix products, on_device(): partial = jnp.dot(full_tokens, masked, preferred_element_type=jnp.float32)  13.5 us
  transfers between devices with their start and end apart: 5, of which 4 were waited for; matrix products, arithmetic and copies ran while one was open for 27% of the time, Pallas kernels for 0%

profile of v1, /device:TPU:0, one launch (start us, length us, event | category | flops | bytes accessed | tf_op | source)
XLA Modules:
  0.0 239.8 jit_solution(18035669964082318997)
XLA Ops:
  7.2 0.7 all-gather.2.cloned.1.call-update
  8.6 0.7 broadcast_subtract_fusion.1
  9.3 0.7 broadcast_subtract_fusion
  9.9 0.8 convolution_compare_fusion
  10.8 0.8 copy.9
  11.6 22.5 %copy.10 = bf16[2048,4096]{0,1:T(8,128)(2,1)} copy(bf16[2048,4096]{1,0:T(8,128)(2,1)} %param.7) | data formatting | bytes 33554432 | tf_op args[1]
  34.1 23.0 %all-gather.2.cloned.1.call-done = bf16[384,2048]{1,0:T(8,128)(2,1)} async-done(((bf16[48,2048]{1,0:T(8,128)(2,1)}), bf16[384,2048]{1,0:T(8,128)(2,1)}) %all-gather.2.cloned.1.call-update) | async-done | bytes 1572880 | tf_op jit(solution)/shard_map/all_gather | solution.py:48
  57.1 26.5 %broadcast_in_dim.29 = pred[16,128,4096]{1,0,2:T(8,128)(4,1)S(1)} broadcast(pred[16,4096]{0,1:T(8,128)(4,1)S(1)} %copy.9), dimensions={0,2} | broadcast | bytes 8454144 | tf_op jit(solution)/shard_map/jit(_where)/broadcast_in_dim | solution.py:47
  83.6 13.5 %fusion.5 = bf16[4096,384]{0,1:T(8,128)(2,1)S(1)} fusion(bf16[384,2048]{1,0:T(8,128)(2,1)S(1)} %copy-done.3, bf16[2048,4096]{0,1:T(8,128)(2,1)} %copy.10, pred[512,8,16,128]{3,2,1,0:T(8,128)(4,1)S(1)} %bitcast.26), kind=kOutput, calls=%fused_computation.8 | convolution fusion | flops 6452412416 | bytes 29884416 | tf_op jit(solution)/shard_map/dot_general | solution.py:49
  97.2 39.6 %all_to_all.10 = bf16[4,96,4096]{2,1,0:T(8,128)(2,1)S(1)} all-to-all(bf16[4,96,4096]{2,1,0:T(8,128)(2,1)S(1)} %bitcast.29), channel_id=1, replica_groups=mesh['row'=8,'col'=4] {'col'}, dimensions={0} | all-to-all | bytes 6291456 | tf_op jit(solution)/shard_map/all_to_all | solution.py:23
  136.8 0.5 convert_reduce_fusion
  137.3 1.5 multiply_convert_fusion
  138.8 11.4 %collective-permute-done = bf16[96,4096]{1,0:T(8,128)(2,1)S(1)} collective-permute-done((bf16[96,4096]{1,0:T(8,128)(2,1)S(1)}, bf16[96,4096]{1,0:T(8,128)(2,1)S(1)}, u32[]{:S(2)}, u32[]{:S(2)}) %collective-permute-start) | collective-permute-done | bytes 786464 | tf_op jit(solution)/shard_map/ppermute | solution.py:14
  150.3 11.4 %collective-permute-done.1 = bf16[96,4096]{1,0:T(8,128)(2,1)S(1)} collective-permute-done((bf16[96,4096]{1,0:T(8,128)(2,1)S(1)}, bf16[96,4096]{1,0:T(8,128)(2,1)S(1)}, u32[]{:S(2)}, u32[]{:S(2)}) %collective-permute-start.1) | collective-permute-done | bytes 786464 | tf_op jit(solution)/shard_map/ppermute | solution.py:14
  161.7 11.4 %collective-permute-done.2 = bf16[96,4096]{1,0:T(8,128)(2,1)S(1)} collective-permute-done((bf16[96,4096]{1,0:T(8,128)(2,1)S(1)}, bf16[96,4096]{1,0:T(8,128)(2,1)S(1)}, u32[]{:S(2)}, u32[]{:S(2)}) %collective-permute-start.2) | collective-permute-done | bytes 786464 | tf_op jit(solution)/shard_map/ppermute | solution.py:14
  173.2 0.1 constant_dynamic-update-slice_fusion.6
  173.2 0.1 constant_dynamic-update-slice_fusion.5
  173.3 0.1 constant_dynamic-update-slice_fusion.4
  173.4 0.1 constant_dynamic-update-slice_fusion.2
  173.6 15.5 %fusion.7 = bf16[384,2048]{1,0:T(8,128)(2,1)} fusion(bf16[2048,4096]{0,1:T(8,128)(2,1)} %copy.10, pred[512,8,16,128]{3,2,1,0:T(8,128)(4,1)} %bitcast.27, bf16[768,4096]{1,0:T(8,128)(2,1)S(1)} %constant_dynamic-update-slice_fusion, s32[]{:T(128)S(6)} %select_n.35), kind=kOutput, calls=%fused_computation.11 | convolution fusion | flops 6451625984 | bytes 29884420 | tf_op jit(solution)/shard_map/dot_general | solution.py:56
  189.1 3.6 %all-to-all-start.1 = ((bf16[8,48,2048]{2,1,0:T(8,128)(2,1)}), bf16[8,48,2048]{2,1,0:T(8,128)(2,1)S(1)}, u32[]{:S(2)}, u32[]{:S(2)}) async-start(bf16[8,48,2048]{2,1,0:T(8,128)(2,1)} %bitcast.5), calls=%async_computation.1 | async-start | bytes 3145728 | tf_op jit(solution)/shard_map/all_to_all | solution.py:23
  192.7 18.1 %fusion = bf16[2048,4096]{0,1:T(8,128)(2,1)} fusion(pred[512,8,16,128]{3,2,1,0:T(8,128)(4,1)} %bitcast.28, bf16[384,2048]{1,0:T(8,128)(2,1)S(1)} %copy-done.4, bf16[768,4096]{1,0:T(8,128)(2,1)} %copy-done.2, s32[]{:T(128)S(6)} %select_n.35), kind=kOutput, calls=%fused_computation.1 | convolution fusion | flops 6459228160 | bytes 29884420 | tf_op jit(solution)/shard_map/dot_general | solution.py:60
  210.8 21.2 %copy.11 = bf16[2048,4096]{1,0:T(8,128)(2,1)} copy(bf16[2048,4096]{0,1:T(8,128)(2,1)} %fusion) | data formatting | bytes 33554432
  232.0 0.9 reduce_sum.22
  (21 shorter events, 0.3 us)
Async XLA Ops:
  7.2 49.9 %all-gather.2.cloned.1.call-start = ((), (), s32[]{:S(2)}) async-start(), calls=%async_computation.2 | async-start | bytes 1769472 | tf_op jit(solution)/shard_map/all_gather | solution.py:48
  57.1 26.5 %copy-start.3 = (bf16[384,2048]{1,0:T(8,128)(2,1)S(1)}, bf16[384,2048]{1,0:T(8,128)(2,1)}, u32[]{:S(2)}) copy-start(bf16[384,2048]{1,0:T(8,128)(2,1)} %all-gather.2.cloned.1.call-done) | copy-start | bytes 4718596
  83.6 13.6 %copy-start = (pred[16,128,4096]{1,0,2:T(8,128)(4,1)}, pred[16,128,4096]{1,0,2:T(8,128)(4,1)S(1)}, u32[]{:S(2)}) copy-start(pred[16,128,4096]{1,0,2:T(8,128)(4,1)S(1)} %broadcast_in_dim.29) | copy-start | bytes 25165828
  97.2 40.1 %copy-start.1 = (bf16[96,4096]{1,0:T(8,128)(2,1)S(1)}, bf16[96,4096]{1,0:T(8,128)(2,1)}, u32[]{:S(2)}) copy-start(bf16[96,4096]{1,0:T(8,128)(2,1)} %param.11) | copy-start | bytes 2359300
  138.8 11.4 %collective-permute-start = (bf16[96,4096]{1,0:T(8,128)(2,1)S(1)}, bf16[96,4096]{1,0:T(8,128)(2,1)S(1)}, u32[]{:S(2)}, u32[]{:S(2)}) collective-permute-start(bf16[96,4096]{1,0:T(8,128)(2,1)S(1)} %get-tuple-element.6), channel_id=1, source_target_pairs={{0,1},{1,2},{2,3},{3,0},{4,5},{5,6},{6,7},{7,4},{8,9},{9,10},{10,1... | collective-permute-start | bytes 2359304 | tf_op jit(solution)/shard_map/ppermute | solution.py:14
  150.3 11.4 %collective-permute-start.1 = (bf16[96,4096]{1,0:T(8,128)(2,1)S(1)}, bf16[96,4096]{1,0:T(8,128)(2,1)S(1)}, u32[]{:S(2)}, u32[]{:S(2)}) collective-permute-start(bf16[96,4096]{1,0:T(8,128)(2,1)S(1)} %collective-permute-done), channel_id=1, source_target_pairs={{0,1},{1,2},{2,3},{3,0},{4,5},{5,6},{6,7},{7,4},{8,9},{9,10},{10,1... | collective-permute-start | bytes 2359304 | tf_op jit(solution)/shard_map/ppermute | solution.py:14
  161.7 11.4 %collective-permute-start.2 = (bf16[96,4096]{1,0:T(8,128)(2,1)S(1)}, bf16[96,4096]{1,0:T(8,128)(2,1)S(1)}, u32[]{:S(2)}, u32[]{:S(2)}) collective-permute-start(bf16[96,4096]{1,0:T(8,128)(2,1)S(1)} %collective-permute-done.1), channel_id=1, source_target_pairs={{0,1},{1,2},{2,3},{3,0},{4,5},{5,6},{6,7},{7,4},{8,9},{9,10},{10,1... | collective-permute-start | bytes 2359304 | tf_op jit(solution)/shard_map/ppermute | solution.py:14
  173.6 15.5 %copy-start.2 = (bf16[768,4096]{1,0:T(8,128)(2,1)}, bf16[768,4096]{1,0:T(8,128)(2,1)S(1)}, u32[]{:S(2)}) copy-start(bf16[768,4096]{1,0:T(8,128)(2,1)S(1)} %constant_dynamic-update-slice_fusion) | copy-start | bytes 18874372
  173.6 19.1 %copy-start.4 = (bf16[384,2048]{1,0:T(8,128)(2,1)S(1)}, bf16[384,2048]{1,0:T(8,128)(2,1)}, u32[]{:S(2)}) copy-start(bf16[384,2048]{1,0:T(8,128)(2,1)} %all-gather.2.cloned.1.call-done) | copy-start | bytes 4718596
  189.1 42.9 %all-to-all-start.1 = ((bf16[8,48,2048]{2,1,0:T(8,128)(2,1)}), bf16[8,48,2048]{2,1,0:T(8,128)(2,1)S(1)}, u32[]{:S(2)}, u32[]{:S(2)}) async-start(bf16[8,48,2048]{2,1,0:T(8,128)(2,1)} %bitcast.5), calls=%async_computation.1 | async-start | bytes 3145728 | tf_op jit(solution)/shard_map/all_to_all | solution.py:23
Sparse Core Ops, SparseCore 0:
  10.2 46.8 all-gather.1
